TPU v7x, 32 devices: a whole 2x2x4 slice. The times are simulated.
32 devices in a mesh: slab: 8 (over z, core), row: 4 (over y, x).
Axes of the slice: x: 2, y: 2, z: 4, core: 2. Of those that a mesh axis runs over, the one named last changes fastest.
Arguments:
- propagator_matrices: float32 [16, 512, 512], P('slab', 'row'), may hold values from -1 to 2
- gain: float32 [512, 128], replicated, may hold values from -0.0546875 to 0.0546875
- obs_matrix: float32 [128, 512], replicated, may hold values from -0.25 to 0.25
- observations: float32 [16, 128], P('slab'), may hold values from -6 to 6
- present: int32 [16], P('slab'), may hold values 0 or 1
- initial: float32 [512], replicated, may hold values from -6 to 6
- smoother_gain: float32 [512, 512], P('row'), may hold values from -1 to 2
Outputs:
- filtered: float32 [16, 512], P('slab')
- smoothed: float32 [16, 512], P('slab')
All inputs are finite; a program needn't handle non-finite values. No bound on the sum of `present` on one device may be relied on, other than what follows from the above.
Results may differ from a plain program's by a relative error of at most 0.00015.
Values sent between devices are 32-bit elements; how exact they have to be, the bound alone decides.
No kernel may reach another device: no remote copies, remote signals or barrier semaphores. Data moves between devices by JAX's collectives and lax.ppermute only.
A program may use at most 192 MiB of HBM per device.

v0:
```python
import jax
import jax.numpy as jnp
from jax import lax
from jax.sharding import PartitionSpec as P


def carried_in(part, axis, combine, identity, reverse):
    count = lax.axis_size(axis)
    place = lax.axis_index(axis)
    ahead = count - 1 - place if reverse else place
    gathered = jax.tree.map(lambda a: lax.all_gather(a, axis), part)
    state = jax.tree.map(lambda a, e: jnp.zeros_like(a) + jnp.asarray(e, a.dtype), part, identity)

    def one(step, state):
        source = count - 1 - step if reverse else step
        return combine(
            state, jax.tree.map(lambda a: lax.dynamic_index_in_dim(a, source, 0, False), gathered)
        )

    return lax.fori_loop(0, ahead, one, state)


def compose(earlier, later):
    greatest_accuracy = lax.Precision.HIGHEST
    return (
        jnp.dot(later[0], earlier[0], precision=greatest_accuracy),
        jnp.dot(later[0], earlier[1], precision=greatest_accuracy) + later[1],
    )


def on_device(propagator_matrices, gain, obs_matrix, observations, present, initial, smoother_gain):
    greatest_accuracy = lax.Precision.HIGHEST
    part_rows = propagator_matrices.shape[1]
    width = propagator_matrices.shape[2]
    epochs_per_group = propagator_matrices.shape[0]
    coupling = jnp.dot(gain, obs_matrix, precision=greatest_accuracy)
    weights = present.astype(jnp.float32)
    drive = jnp.einsum("so,do->sd", observations, gain, precision=greatest_accuracy)
    full_trans, full_smooth = (
        lax.all_gather(propagator_matrices, "row", axis=1, tiled=True),
        lax.all_gather(smoother_gain, "row", axis=0, tiled=True),
    )

    def forward(state, inputs):
        matrix, forced_response, weight = inputs
        pred = jnp.dot(matrix, state, precision=greatest_accuracy)
        new_state = pred + weight * (
            forced_response - jnp.dot(coupling, pred, precision=greatest_accuracy)
        )
        return (new_state, (new_state, new_state - pred))

    def backward(carried, term):
        new_carried = jnp.dot(full_smooth, carried, precision=greatest_accuracy) + term
        return (new_carried, new_carried)

    zeros = jnp.zeros((width,), jnp.float32)
    identity = jnp.eye(width, dtype=jnp.float32)
    local_offset, _ = lax.scan(forward, zeros, (full_trans, drive, weights))
    row_start = lax.axis_index("row") * part_rows
    row_ids = lax.broadcasted_iota(jnp.int32, (part_rows, width), 0) + row_start
    col_ids = lax.broadcasted_iota(jnp.int32, (part_rows, width), 1)
    unit_matrix_lines = (row_ids == col_ids).astype(jnp.float32)

    def postmultiply_operator(carry, inputs):
        matrix, weight = inputs
        mixed = carry - weight * jnp.dot(carry, coupling, precision=greatest_accuracy)
        return (jnp.dot(mixed, matrix, precision=greatest_accuracy), None)

    map_rows, _ = lax.scan(
        postmultiply_operator, unit_matrix_lines, (full_trans, weights), reverse=True
    )
    power_rows = lax.fori_loop(
        0,
        epochs_per_group - 1,
        lambda index, acc: jnp.dot(acc, full_smooth, precision=greatest_accuracy),
        smoother_gain,
    )
    slab_map, power = (
        lax.all_gather(map_rows, "row", axis=0, tiled=True),
        lax.all_gather(power_rows, "row", axis=0, tiled=True),
    )
    prefix_map, prefix_offset = carried_in(
        (slab_map, local_offset), "slab", compose, (identity, zeros), False
    )
    start_state = jnp.dot(prefix_map, initial, precision=greatest_accuracy) + prefix_offset
    _, (filtered, correction) = lax.scan(forward, start_state, (full_trans, drive, weights))
    local_carried, _ = lax.scan(backward, zeros, correction, reverse=True)
    _, next_carried = carried_in((power, local_carried), "slab", compose, (identity, zeros), True)
    _, carried = lax.scan(backward, next_carried, correction, reverse=True)
    smoothed = filtered + carried - correction
    return (filtered, smoothed)


def solution(mesh):
    placed = (P("slab", "row", None), P(), P(), P("slab", None), P("slab"), P(), P("row", None))
    return jax.shard_map(
        on_device,
        mesh=mesh,
        in_specs=placed,
        out_specs=(P("slab", None), P("slab", None)),
        check_vma=False,
    )
```

profile of v0, /device:TPU:0, one launch (start us, length us, event | category | flops | bytes accessed | tf_op | source)
XLA Modules:
  0.0 324.6 jit_solution(9640601542221443507)
XLA Ops:
  7.2 0.7 all-gather.13.cloned.1.call-update
  7.9 0.0 all-gather.17.cloned.1.call-start
  8.0 0.7 all-gather.17.cloned.1.call-update
  8.7 0.0 all-gather.15.cloned.1.call-start
  8.7 0.7 convert_element_type.11
  9.4 0.1 fusion.30
  9.5 1.9 fusion.34
  11.4 36.5 %all-gather.13.cloned.1.call-done = f32[2,512,512]{2,1,0:T(8,128)} async-done(((f32[2,128,512]{2,1,0:T(8,128)}), f32[2,512,512]{2,1,0:T(8,128)}) %all-gather.13.cloned.1.call-update) | async-done | bytes 2097168 | tf_op jit(solution)/shard_map/all_gather | solution.py:40
  47.9 7.8 %while.100 = (s32[]{:T(128)}, f32[128,512]{1,0:T(8,128)S(1)}, f32[2]{0:T(128)S(1)}, f32[512,512]{1,0:T(8,128)S(1)}, f32[2,512,512]{2,1,0:T(8,128)}, /*index=5*/s32[]{:T(128)}) while((s32[]{:T(128)}, f32[128,512]{1,0:T(8,128)S(1)}, f32[2]{0:T(128)S(1)}, f32[512,512]{1,0:T(8,128)S(1)}, f32[2,512,512]{2,1,0:T(8,128)}, /*index=5*/s32[]{:T(128)}) %tuple.172), condition=%wide.region_1.2_spmd, body=%wide.region_0.1_spmd.sunk | while | flops 805437440 | bytes 3145829 | solution.py:69
  47.9 0.6 dynamic_slice.131
  48.5 1.4 fusion.98
  49.9 1.9 fusion.99
  51.8 0.6 dynamic_slice.131
  52.4 1.4 fusion.98
  53.8 1.9 fusion.99
  55.7 0.7 copy-done.2
  56.5 0.0 all-gather.19.cloned.1.call-start
  56.5 19.9 %all-gather.17.cloned.1.call-done = f32[512,512]{1,0:T(8,128)} async-done(((f32[128,512]{1,0:T(8,128)}), f32[512,512]{1,0:T(8,128)}) %all-gather.17.cloned.1.call-update) | async-done | bytes 1048592 | tf_op jit(solution)/shard_map/all_gather | solution.py:41
  76.4 2.6 fusion.37
  79.1 0.0 all-gather.21.cloned.1.call-start
  79.1 25.8 %all-gather.15.cloned.1.call-done = f32[512,512]{1,0:T(8,128)} async-done(((f32[128,512]{1,0:T(8,128)}), f32[512,512]{1,0:T(8,128)}) %all-gather.15.cloned.1.call-update) | async-done | bytes 1048592 | tf_op jit(solution)/shard_map/all_gather | solution.py:79
  104.9 0.0 all-gather.23.cloned.1.call-start
  105.0 28.3 %all-gather.19.cloned.1.call-done = f32[512,512]{1,0:T(8,128)} async-done(((f32[128,512]{1,0:T(8,128)}), f32[512,512]{1,0:T(8,128)}) %all-gather.19.cloned.1.call-update) | async-done | bytes 1048592 | tf_op jit(solution)/shard_map/all_gather | solution.py:80
  133.3 0.1 fusion.29
  133.4 0.3 fusion.35
  133.8 9.1 %while.105 = (s32[]{:T(128)}, f32[512]{0:T(512)S(1)}, f32[2,512,512]{2,1,0:T(8,128)}, f32[2]{0:T(128)S(1)}, f32[2,512]{1,0:T(2,128)S(1)}, /*index=5*/f32[512,512]{1,0:T(8,128)S(1)}, s32[]{:T(128)}, s32[]{:T(128)}) while((s32[]{:T(128)}, f32[512]{0:T(512)S(1)}, f32[2,512,512]{2,1,0:T(8,128)}, f32[2]{0:T(128)S(1)}, ...), condition=%wide.region_3.4_spmd.clone, body=%wide.region_2.3_spmd.clone.sunk | while | flops 6293507 | bytes 2122355 | solution.py:58
  133.8 2.2 fusion.123
  136.0 1.0 fusion.124
  137.0 0.7 dynamic_slice.143
  137.6 0.7 multiply_add_fusion.4
  138.3 2.2 fusion.123
  140.6 1.0 fusion.124
  141.6 0.7 dynamic_slice.143
  142.2 0.7 multiply_add_fusion.4
  142.9 12.9 %all-gather.4 = f32[8,1,512]{2,1,0:T(1,128)S(1)} all-gather(f32[1,1,512]{2,1,0:T(1,128)S(1)} %bitcast.205), channel_id=3, replica_groups=mesh['slab'=8,'row'=4] {'slab'}, dimensions={0}, use_global_device_ids=true | all-gather | bytes 18432 | tf_op jit(solution)/shard_map/all_gather | solution.py:11
  155.8 61.1 %all-gather.21.cloned.1.call-done = f32[4096,512]{1,0:T(8,128)} async-done(((f32[512,512]{1,0:T(8,128)}), f32[4096,512]{1,0:T(8,128)}) %all-gather.21.cloned.1.call-update) | async-done | bytes 8388624 | tf_op jit(solution)/shard_map/all_gather | solution.py:11
  216.9 0.7 copy-done.5
  217.6 1.0 fusion.36
  218.6 9.2 %while.102 = (s32[]{:T(128)}, f32[512]{0:T(512)S(1)}, f32[2,512]{1,0:T(2,128)S(1)}, f32[2,512]{1,0:T(2,128)S(1)}, f32[2,512,512]{2,1,0:T(8,128)}, /*index=5*/f32...) while((s32[]{:T(128)}, f32[512]{0:T(512)S(1)}, ...), condition=%wide.region_7.8_spmd, body=%wide.region_6.7_spmd.sunk | while | flops 6293506 | bytes 2128513 | solution.py:86
  218.7 2.2 fusion.110
  220.9 1.0 fusion.111
  221.9 0.6 dynamic_slice.137
  222.4 0.7 fusion.112
  223.2 2.3 fusion.110
  225.5 1.0 fusion.111
  226.5 0.6 dynamic_slice.137
  227.1 0.7 fusion.112
  227.9 2.1 while.106
  227.9 1.0 fusion.127
  228.9 1.0 fusion.127
  230.0 47.5 %all-gather.5 = f32[8,1,512]{2,1,0:T(1,128)S(1)} all-gather(f32[1,1,512]{2,1,0:T(1,128)S(1)} %bitcast.204), channel_id=5, replica_groups=mesh['slab'=8,'row'=4] {'slab'}, dimensions={0}, use_global_device_ids=true | all-gather | bytes 18432 | tf_op jit(solution)/shard_map/all_gather | solution.py:11
  277.5 21.7 %all-gather.23.cloned.1.call-done = f32[4096,512]{1,0:T(8,128)} async-done(((f32[512,512]{1,0:T(8,128)}), f32[4096,512]{1,0:T(8,128)}) %all-gather.23.cloned.1.call-update) | async-done | bytes 8388624 | tf_op jit(solution)/shard_map/all_gather | solution.py:11
  299.1 15.8 %while.103 = (s32[]{:T(128)}, f32[512]{0:T(512)S(1)}, s32[]{:T(128)}, f32[8,512,512]{2,1,0:T(8,128)}, f32[8,512]{1,0:T(8,128)S(1)}, /*index=5*/s32[]{:T(128)}, s32[]{:T(128)}, s32[]{:T(128)}, s32[]{:T(128)}) while((s32[]{:T(128)}, f32[512]{0:T(512)S(1)}, s32[]{:T(128)}, f32[8,512,512]{2,1,0:T(8,128)}, f32[8,512]{1,0:T(8,128)S(1)}, ...), condition=%wide.region_11.12_spmd, body=%wide.region_10.11_spmd.sunk | while | flops 3146246 | bytes 1063059 | solution.py:20
  299.1 2.2 fusion.115
  301.4 2.2 fusion.115
  303.6 2.2 fusion.115
  305.9 2.2 fusion.115
  308.2 2.2 fusion.115
  310.4 2.2 fusion.115
  312.7 2.2 fusion.115
  315.0 2.1 while.104
  315.0 1.0 fusion.118
  316.1 1.0 fusion.118
  317.1 0.6 add_subtract_fusion
  (65 shorter events, 0.7 us)
Async XLA Ops:
  7.2 2.3 copy-start
  7.2 40.7 %all-gather.13.cloned.1.call-start = ((), (), s32[]{:S(2)}) async-start(), calls=%async_computation | async-start | bytes 2621440 | tf_op jit(solution)/shard_map/all_gather | solution.py:40
  7.9 68.5 %all-gather.17.cloned.1.call-start = ((), (), s32[]{:S(2)}) async-start(), calls=%async_computation.2 | async-start | bytes 1310720 | tf_op jit(solution)/shard_map/all_gather | solution.py:41
  8.7 96.3 %all-gather.15.cloned.1.call-start = ((), (), s32[]{:S(2)}) async-start(), calls=%async_computation.1 | async-start | bytes 1310720 | tf_op jit(solution)/shard_map/all_gather | solution.py:79
  11.4 65.0 %copy-start.3 = (f32[128,512]{1,0:T(8,128)S(1)}, f32[128,512]{1,0:T(8,128)}, u32[]{:S(2)}) copy-start(f32[128,512]{1,0:T(8,128)} %param.27) | copy-start | bytes 786436
  47.9 85.5 %copy-start.6 = (f32[2,128]{1,0:T(2,128)S(1)}, f32[2,128]{1,0:T(2,128)}, u32[]{:S(2)}) copy-start(f32[2,128]{1,0:T(2,128)} %param.24) | copy-start | bytes 3076
  55.7 0.7 copy-start.2
  56.5 76.8 %all-gather.19.cloned.1.call-start = ((), (), s32[]{:S(2)}) async-start(), calls=%async_computation.3 | async-start | bytes 1310720 | tf_op jit(solution)/shard_map/all_gather | solution.py:80
  79.1 137.9 %all-gather.21.cloned.1.call-start = ((), (), s32[]{:S(2)}) async-start(), calls=%async_computation.4 | async-start | bytes 9437184 | tf_op jit(solution)/shard_map/all_gather | solution.py:11
  104.9 194.2 %all-gather.23.cloned.1.call-start = ((), (), s32[]{:S(2)}) async-start(), calls=%async_computation.5 | async-start | bytes 9437184 | tf_op jit(solution)/shard_map/all_gather | solution.py:11
  216.9 0.7 copy-start.5
  216.9 10.9 %copy-start.1 = (f32[512,512]{1,0:T(8,128)S(1)}, f32[512,512]{1,0:T(8,128)}, u32[]{:S(2)}) copy-start(f32[512,512]{1,0:T(8,128)} %all-gather.17.cloned.1.call-done) | copy-start | bytes 3145732
  227.8 89.9 %copy-start.4 = (f32[2,512]{1,0:T(2,128)}, f32[2,512]{1,0:T(2,128)S(1)}, u32[]{:S(2)}) copy-start(f32[2,512]{1,0:T(2,128)S(1)} %get-tuple-element.492) | copy-start | bytes 12292
Sparse Core Ops, SparseCore 0:
  9.9 38.0 all-gather.12
  49.7 26.6 all-gather.16
  78.3 26.6 all-gather.14
  106.6 26.6 all-gather.18
  134.7 82.1 all-gather.20
  218.4 80.6 all-gather.22
where the time goes:
time: 326 us; the launch traced here: 325 us
  waiting for transfers between devices  195 us (60%)
  blocking collectives  60.4 us (19%)
  matrix products  44.6 us (14%)
  between operations  14.3 us (4%)
  local copies, waits for them, and re-layouts  5.58 us (2%)
  other arithmetic  4.22 us (1%)
    all_gather x2, waiting for transfers between devices, carried_in(): gathered = jax.tree.map(lambda a: lax.all_gather(a, axis), part)  82.7 us
    all_gather x2, blocking collectives, carried_in(): gathered = jax.tree.map(lambda a: lax.all_gather(a, axis), part)  60.4 us
    all_gather x1, waiting for transfers between devices, on_device(): lax.all_gather(propagator_matrices, 'row', axis=1, tiled=True)  36.5 us
    all_gather x1, waiting for transfers between devices, on_device(): lax.all_gather(power_rows, 'row', axis=0, tiled=True)  28.3 us
    all_gather x1, waiting for transfers between devices, on_device(): lax.all_gather(map_rows, 'row', axis=0, tiled=True)  25.8 us
    all_gather x1, waiting for transfers between devices, on_device(): lax.all_gather(smoother_gain, 'row', axis=0, tiled=True)  19.9 us
    dot_general x7, matrix products, compose(): jnp.dot(later[0], earlier[1], precision=greatest_accuracy) + later[1]  15.4 us
    dot_general x4, matrix products, forward(): pred = jnp.dot(matrix, state, precision=greatest_accuracy)  8.93 us
  transfers between devices with their start and end apart: 6, of which 6 were waited for; matrix products, arithmetic and copies ran while one was open for 11% of the time, Pallas kernels for 0%

commit v1 on v0

--- a/solution.py
+++ b/solution.py
@@ -2,6 +2,27 @@
 import jax.numpy as jnp
 from jax import lax
 from jax.sharding import PartitionSpec as P
+
+
+def ring_gather(array, axis, dim):
+    size, index, rows = (lax.axis_size(axis), lax.axis_index(axis), array.shape[dim])
+    upward = [(i, (i + 1) % size) for i in range(size)]
+    left = [(i, (i - 1) % size) for i in range(size)]
+    whole = jnp.zeros((*array.shape[:dim], size * rows, *array.shape[dim + 1 :]), array.dtype)
+    whole = lax.dynamic_update_slice_in_dim(whole, array, index * rows, axis=dim)
+    from_left = from_right = array
+    middle = size // 2
+    for step in range(1, middle + 1):
+        from_left = lax.ppermute(from_left, axis, upward)
+        whole = lax.dynamic_update_slice_in_dim(
+            whole, from_left, (index - step) % size * rows, axis=dim
+        )
+        if step < size - middle:
+            from_right = lax.ppermute(from_right, axis, left)
+            whole = lax.dynamic_update_slice_in_dim(
+                whole, from_right, (index + step) % size * rows, axis=dim
+            )
+    return whole
 
 
 def carried_in(part, axis, combine, identity, reverse):
@@ -37,7 +58,7 @@
     weights = present.astype(jnp.float32)
     drive = jnp.einsum("so,do->sd", observations, gain, precision=greatest_accuracy)
     full_trans, full_smooth = (
-        lax.all_gather(propagator_matrices, "row", axis=1, tiled=True),
+        ring_gather(propagator_matrices, "row", 1),
         lax.all_gather(smoother_gain, "row", axis=0, tiled=True),
     )
 

time: 326 us -> 313 us (0.960)
  waiting for transfers between devices: 195 us -> 157 us
  blocking collectives: 60.4 us -> 75.2 us
  starting transfers between devices: 0.23 us -> 6.69 us
    all_gather x1 -> x0, waiting for transfers between devices: 36.5 us -> none  [on_device(): lax.all_gather(propagator_matrices, 'row', axis=1, tiled=True)]
    ppermute x0 -> x3, waiting for transfers between devices: none -> 35.2 us  [the longest x2 23.2 us: ring_gather(): from_left = lax.ppermute(from_left, axis, upward)]
    all_gather x1, waiting for transfers between devices: 19.9 us -> 0.02 us  [on_device(): lax.all_gather(smoother_gain, 'row', axis=0, tiled=True)]
    all_gather x2, blocking collectives: 60.4 us -> 75.2 us  [carried_in(): gathered = jax.tree.map(lambda a: lax.all_gather(a, axis), part)]
    all_gather x2, waiting for transfers between devices: 82.7 us -> 68.4 us  [carried_in(): gathered = jax.tree.map(lambda a: lax.all_gather(a, axis), part)]
    ppermute x0 -> x3, starting transfers between devices: none -> 6.49 us  [the longest x2 5.47 us: ring_gather(): from_left = lax.ppermute(from_left, axis, upward)]
    dot_general x4, matrix products: 8.93 us -> 3.97 us  [forward(): pred = jnp.dot(matrix, state, precision=greatest_accuracy)]
    dynamic_update_slice x0 -> x4, local copies, waits for them, and re-layouts: none -> 3.28 us  [the longest x2 2.15 us: ring_gather(): lax.dynamic_update_slice_in_dim(whole, from_left, (index - step) % size *...]
  transfers between devices with their start and end apart: 6 -> 8, of which waited for: 6 -> 7; matrix products, arithmetic and copies ran while one was open for 11% -> 13% of each run, Pallas kernels for 0% -> 0%
where the time goes in v1:
time: 313 us; the launch traced here: 311 us
  waiting for transfers between devices  157 us (50%)
  blocking collectives  75.2 us (24%)
  matrix products  44.7 us (14%)
  between operations  14 us (4%)
  local copies, waits for them, and re-layouts  8.33 us (3%)
  starting transfers between devices  6.69 us (2%)
  other arithmetic  5.2 us (2%)
    all_gather x2, blocking collectives, carried_in(): gathered = jax.tree.map(lambda a: lax.all_gather(a, axis), part)  75.2 us
    all_gather x2, waiting for transfers between devices, carried_in(): gathered = jax.tree.map(lambda a: lax.all_gather(a, axis), part)  68.4 us
    all_gather x1, waiting for transfers between devices, on_device(): lax.all_gather(power_rows, 'row', axis=0, tiled=True)  28.4 us
    all_gather x1, waiting for transfers between devices, on_device(): lax.all_gather(map_rows, 'row', axis=0, tiled=True)  24.5 us
    ppermute x2, waiting for transfers between devices, ring_gather(): from_left = lax.ppermute(from_left, axis, upward)  23.2 us
    dot_general x7, matrix products, compose(): jnp.dot(later[0], earlier[1], precision=greatest_accuracy) + later[1]  15.5 us
    ppermute x1, waiting for transfers between devices, ring_gather(): from_right = lax.ppermute(from_right, axis, left)  12 us
    dot_general x4, matrix products, backward(): jnp.dot(full_smooth, carried, precision=greatest_accuracy) + term  6.45 us
  transfers between devices with their start and end apart: 8, of which 7 were waited for; matrix products, arithmetic and copies ran while one was open for 13% of the time, Pallas kernels for 0%

profile of v1, /device:TPU:0, one launch (start us, length us, event | category | flops | bytes accessed | tf_op | source)
XLA Modules:
  0.0 311.3 jit_solution(8508995134935546654)
XLA Ops:
  7.2 3.0 collective-permute-start
  10.2 1.0 collective-permute-start.1
  11.3 2.0 fusion.34
  13.3 0.2 broadcast_in_dim.23
  13.7 11.3 %collective-permute-done = f32[2,128,512]{2,1,0:T(8,128)} collective-permute-done((f32[2,128,512]{2,1,0:T(8,128)}, f32[2,128,512]{2,1,0:T(8,128)}, u32[]{:S(2)}, u32[]{:S(2)}) %collective-permute-start) | collective-permute-done | bytes 524320 | tf_op jit(solution)/shard_map/ppermute | solution.py:16
  25.0 2.5 collective-permute-start.2
  27.5 0.8 fusion.30
  28.3 1.1 constant_dynamic-update-slice_fusion.2
  29.4 12.0 %collective-permute-done.1 = f32[2,128,512]{2,1,0:T(8,128)} collective-permute-done((f32[2,128,512]{2,1,0:T(8,128)}, f32[2,128,512]{2,1,0:T(8,128)}, u32[]{:S(2)}, u32[]{:S(2)}) %collective-permute-start.1) | collective-permute-done | bytes 524320 | tf_op jit(solution)/shard_map/ppermute | solution.py:21
  41.4 1.1 constant_dynamic-update-slice_fusion.1
  42.5 11.8 %collective-permute-done.2 = f32[2,128,512]{2,1,0:T(8,128)} collective-permute-done((f32[2,128,512]{2,1,0:T(8,128)}, f32[2,128,512]{2,1,0:T(8,128)}, u32[]{:S(2)}, u32[]{:S(2)}) %collective-permute-start.2) | collective-permute-done | bytes 524320 | tf_op jit(solution)/shard_map/ppermute | solution.py:16
  54.3 1.1 constant_dynamic-update-slice_fusion
  55.4 8.9 %while.100 = (s32[]{:T(128)}, f32[128,512]{1,0:T(8,128)}, f32[2]{0:T(128)S(1)}, f32[512,512]{1,0:T(8,128)S(1)}, f32[2,512,512]{2,1,0:T(8,128)S(1)}, /*index=5*/s32[]{:T(128)}) while((s32[]{:T(128)}, f32[128,512]{1,0:T(8,128)}, f32[2]{0:T(128)S(1)}, f32[512,512]{1,0:T(8,128)S(1)}, f32[2,512,512]{2,1,0:T(8,128)S(1)}, /*index=5*/s32[]{:T(128)}) %tuple.172), condition=%wide.region_1.2_spmd, body=%wide.region_0.1_spmd.sunk | while | flops 805437440 | bytes 3145829 | solution.py:90
  55.4 0.6 dynamic_slice.131
  56.0 2.4 fusion.98
  58.4 1.5 fusion.99
  59.9 0.6 dynamic_slice.131
  60.4 2.4 fusion.98
  62.8 1.5 fusion.99
  64.3 0.0 all-gather.16.cloned.1.call-start
  64.4 2.7 fusion.37
  67.2 24.5 %all-gather.12.cloned.1.call-done = f32[512,512]{1,0:T(8,128)} async-done(((f32[128,512]{1,0:T(8,128)}), f32[512,512]{1,0:T(8,128)}) %all-gather.12.cloned.1.call-update) | async-done | bytes 1048592 | tf_op jit(solution)/shard_map/all_gather | solution.py:100
  91.7 28.4 %all-gather.16.cloned.1.call-done = f32[512,512]{1,0:T(8,128)} async-done(((f32[128,512]{1,0:T(8,128)}), f32[512,512]{1,0:T(8,128)}) %all-gather.16.cloned.1.call-update) | async-done | bytes 1048592 | tf_op jit(solution)/shard_map/all_gather | solution.py:101
  120.2 1.1 fusion.29
  121.3 0.3 fusion.35
  121.6 6.5 %while.105 = (s32[]{:T(128)}, f32[512]{0:T(512)S(1)}, f32[2,512,512]{2,1,0:T(8,128)S(1)}, f32[2]{0:T(128)S(1)}, f32[2,512]{1,0:T(2,128)S(1)}, /*index=5*/f32[512,512]{1,0:T(8,128)S(1)}, s32[]{:T(128)}, s32[]{:T(128)}) while((s32[]{:T(128)}, f32[512]{0:T(512)S(1)}, f32[2,512,512]{2,1,0:T(8,128)S(1)}, f32[2]{0:T(128)S(1)}, ...), condition=%wide.region_3.4_spmd.clone, body=%wide.region_2.3_spmd.clone.sunk | while | flops 6293507 | bytes 2121847 | solution.py:79
  121.6 1.0 fusion.123
  122.6 1.0 fusion.124
  123.6 0.6 dynamic_slice.143
  124.2 0.6 multiply_add_fusion.4
  124.9 1.0 fusion.123
  125.9 1.0 fusion.124
  126.9 0.6 dynamic_slice.143
  127.5 0.6 multiply_add_fusion.4
  128.1 13.2 %all-gather.4 = f32[8,1,512]{2,1,0:T(1,128)S(1)} all-gather(f32[1,1,512]{2,1,0:T(1,128)S(1)} %bitcast.205), channel_id=3, replica_groups=mesh['slab'=8,'row'=4] {'slab'}, dimensions={0}, use_global_device_ids=true | all-gather | bytes 18432 | tf_op jit(solution)/shard_map/all_gather | solution.py:32
  141.4 62.5 %all-gather.18.cloned.1.call-done = f32[4096,512]{1,0:T(8,128)} async-done(((f32[512,512]{1,0:T(8,128)}), f32[4096,512]{1,0:T(8,128)}) %all-gather.18.cloned.1.call-update) | async-done | bytes 8388624 | tf_op jit(solution)/shard_map/all_gather | solution.py:32
  203.9 0.7 copy-done.4
  204.5 2.2 fusion.36
  206.8 6.7 %while.102 = (s32[]{:T(128)}, f32[512]{0:T(512)S(1)}, f32[2,512]{1,0:T(2,128)S(1)}, f32[2,512]{1,0:T(2,128)S(1)}, f32[2,512,512]{2,1,0:T(8,128)S(1)}, /*index=5*...) while((s32[]{:T(128)}, f32[512]{0:T(512)S(1)}, ...), condition=%wide.region_7.8_spmd, body=%wide.region_6.7_spmd.sunk | while | flops 6293506 | bytes 2128005 | solution.py:107
  206.8 1.0 fusion.110
  207.8 1.0 fusion.111
  208.8 0.6 dynamic_slice.137
  209.4 0.7 fusion.112
  210.1 1.0 fusion.110
  211.1 1.0 fusion.111
  212.1 0.6 dynamic_slice.137
  212.7 0.7 fusion.112
  213.5 4.6 %while.106 = (s32[]{:T(128)}, f32[512]{0:T(512)S(1)}, f32[512,512]{1,0:T(8,128)}, f32[2,512]{1,0:T(2,128)S(1)}, s32[]{:T(128)}, /*index=5*/s32[]{:T(128)}) while((s32[]{:T(128)}, f32[512]{0:T(512)S(1)}, f32[512,512]{1,0:T(8,128)}, f32[2,512]{1,0:T(2,128)S(1)}, s32[]{:T(128)}, /*index=5*/s32[]{:T(128)}) %tuple.184), condition=%wide.region_9.10_spmd.clone, body=%wide.region_8.9_spmd.clone.sunk | while | flops 3146756 | bytes 1067103 | solution.py:108
  213.5 2.3 fusion.127
  215.9 2.2 fusion.127
  218.1 62.0 %all-gather.5 = f32[8,1,512]{2,1,0:T(1,128)S(1)} all-gather(f32[1,1,512]{2,1,0:T(1,128)S(1)} %bitcast.204), channel_id=5, replica_groups=mesh['slab'=8,'row'=4] {'slab'}, dimensions={0}, use_global_device_ids=true | all-gather | bytes 18432 | tf_op jit(solution)/shard_map/all_gather | solution.py:32
  280.1 5.9 %all-gather.20.cloned.1.call-done = f32[4096,512]{1,0:T(8,128)} async-done(((f32[512,512]{1,0:T(8,128)}), f32[4096,512]{1,0:T(8,128)}) %all-gather.20.cloned.1.call-update) | async-done | bytes 8388624 | tf_op jit(solution)/shard_map/all_gather | solution.py:32
  286.0 15.9 %while.103 = (s32[]{:T(128)}, f32[512]{0:T(512)S(1)}, s32[]{:T(128)}, f32[8,512,512]{2,1,0:T(8,128)}, f32[8,512]{1,0:T(8,128)S(1)}, /*index=5*/s32[]{:T(128)}, s32[]{:T(128)}, s32[]{:T(128)}, s32[]{:T(128)}) while((s32[]{:T(128)}, f32[512]{0:T(512)S(1)}, s32[]{:T(128)}, f32[8,512,512]{2,1,0:T(8,128)}, f32[8,512]{1,0:T(8,128)S(1)}, ...), condition=%wide.region_11.12_spmd, body=%wide.region_10.11_spmd.sunk | while | flops 3146246 | bytes 1063059 | solution.py:41
  286.0 2.3 fusion.115
  288.4 2.2 fusion.115
  290.6 2.2 fusion.115
  292.9 2.2 fusion.115
  295.2 2.2 fusion.115
  297.4 2.2 fusion.115
  299.7 2.2 fusion.115
  302.0 2.1 while.104
  302.0 1.0 fusion.118
  303.1 1.0 fusion.118
  304.1 0.6 add_subtract_fusion
  (73 shorter events, 0.9 us)
Async XLA Ops:
  7.2 4.2 %copy-start = (f32[512,128]{1,0:T(8,128)S(1)}, f32[512,128]{1,0:T(8,128)}, u32[]{:S(2)}) copy-start(f32[512,128]{1,0:T(8,128)} %param.22) | copy-start | bytes 786436
  7.2 57.2 %all-gather.14.cloned.1.call-start = ((), (), s32[]{:S(2)}) async-start(), calls=%async_computation.1 | async-start | bytes 1310720 | tf_op jit(solution)/shard_map/all_gather | solution.py:62
  7.2 17.8 %collective-permute-start = (f32[2,128,512]{2,1,0:T(8,128)}, f32[2,128,512]{2,1,0:T(8,128)}, u32[]{:S(2)}, u32[]{:S(2)}) collective-permute-start(f32[2,128,512]{2,1,0:T(8,128)} %param.21), channel_id=1, source_target_pairs={{0,1},{1,2},{2,3},{3,0},{4,5},{5,6},{6,7},{7,4},{8,9},{9,10},{10,1... | collective-permute-start | bytes 1572872 | tf_op jit(solution)/shard_map/ppermute | solution.py:16
  10.2 31.2 %collective-permute-start.1 = (f32[2,128,512]{2,1,0:T(8,128)}, f32[2,128,512]{2,1,0:T(8,128)}, u32[]{:S(2)}, u32[]{:S(2)}) collective-permute-start(f32[2,128,512]{2,1,0:T(8,128)} %param.21), channel_id=1, source_target_pairs={{0,3},{1,0},{2,1},{3,2},{4,7},{5,4},{6,5},{7,6},{8,11},{9,8},{10,9... | collective-permute-start | bytes 1572872 | tf_op jit(solution)/shard_map/ppermute | solution.py:21
  11.3 80.4 %all-gather.12.cloned.1.call-start = ((), (), s32[]{:S(2)}) async-start(), calls=%async_computation | async-start | bytes 1310720 | tf_op jit(solution)/shard_map/all_gather | solution.py:100
  11.3 2.3 copy-start.2
  11.3 16.1 %copy-start.6 = (s32[2]{0:T(128)S(1)}, s32[2]{0:T(128)}, u32[]{:S(2)}) copy-start(s32[2]{0:T(128)} %param.25) | copy-start | bytes 28
  25.0 29.3 %collective-permute-start.2 = (f32[2,128,512]{2,1,0:T(8,128)}, f32[2,128,512]{2,1,0:T(8,128)}, u32[]{:S(2)}, u32[]{:S(2)}) collective-permute-start(f32[2,128,512]{2,1,0:T(8,128)} %collective-permute-done), channel_id=1, source_target_pairs={{0,1},{1,2},{2,3},{3,0},{4,5},{5,6},{6,7},{7,4},{8,9},{9,10},{10,1... | collective-permute-start | bytes 1572872 | tf_op jit(solution)/shard_map/ppermute | solution.py:16
  64.3 55.8 %all-gather.16.cloned.1.call-start = ((), (), s32[]{:S(2)}) async-start(), calls=%async_computation.2 | async-start | bytes 1310720 | tf_op jit(solution)/shard_map/all_gather | solution.py:101
  67.1 54.2 %copy-start.5 = (f32[2,128]{1,0:T(2,128)S(1)}, f32[2,128]{1,0:T(2,128)}, u32[]{:S(2)}) copy-start(f32[2,128]{1,0:T(2,128)} %param.24) | copy-start | bytes 3076
  67.2 136.7 %all-gather.18.cloned.1.call-start = ((), (), s32[]{:S(2)}) async-start(), calls=%async_computation.3 | async-start | bytes 9437184 | tf_op jit(solution)/shard_map/all_gather | solution.py:32
  91.7 194.3 %all-gather.20.cloned.1.call-start = ((), (), s32[]{:S(2)}) async-start(), calls=%async_computation.4 | async-start | bytes 9437184 | tf_op jit(solution)/shard_map/all_gather | solution.py:32
  203.9 0.7 copy-start.4
  213.5 90.7 %copy-start.3 = (f32[2,512]{1,0:T(2,128)}, f32[2,512]{1,0:T(2,128)S(1)}, u32[]{:S(2)}) copy-start(f32[2,512]{1,0:T(2,128)S(1)} %get-tuple-element.492) | copy-start | bytes 12292
  286.0 16.0 %copy-start.1 = (f32[512,512]{1,0:T(8,128)S(1)}, f32[512,512]{1,0:T(8,128)}, u32[]{:S(2)}) copy-start(f32[512,512]{1,0:T(8,128)} %get-tuple-element.1041) | copy-start | bytes 3145732
Sparse Core Ops, SparseCore 0:
  11.4 36.3 all-gather.13
  64.4 27.1 all-gather.11
  93.5 26.6 all-gather.15
  121.6 82.2 all-gather.17
  205.3 80.6 all-gather.19
